TPU v7x, 512 devices: a whole 4x4x16 slice. The times are simulated.
512 devices in a mesh: sx: 32 (over z_hi, y, core), sy: 16 (over x, z_lo).
Axes of the slice: x: 4, y: 4, z: 16 (z_hi: 4, z_lo: 4; z = z_hi * 4 + z_lo), core: 2. Of those that a mesh axis runs over, the one named last changes fastest.
Arguments:
- forward_prop: bfloat16 [2, 2, 12, 12, 64, 4096], P(None, None, None, None, 'sx', 'sy'), may hold values from -0.08984375 to 0.08984375
- backward_prop: bfloat16 [2, 2, 12, 12, 64, 4096], P(None, None, None, None, 'sx', 'sy'), may hold values from -0.08984375 to 0.08984375
- gamma_table: int32 [16, 4, 2], replicated, may hold values from 0 to 3, as said below
- source_site: int32 [3], replicated, may hold values from 0 to 63
- momenta: int32 [32, 3], replicated, may hold values from -8 to 7
Outputs:
- corr: float32 [16, 2, 2, 64, 4096], P(None, None, None, 'sx', 'sy')
- listed: float32 [2, 16, 2, 32], replicated
Inputs may be any that keep to these rules, and one draw needn't show every extreme that they name: For every insertion g, gamma_table[g, 0..3, 0] is a permutation of 0..3; gamma_table[g, s, 1] is the power of i of that entry.
All inputs are finite; a program needn't handle non-finite values.
Results may differ from a plain program's by a relative error of at most 0.0003.
Values sent between devices are 32-bit elements; how exact they have to be, the bound alone decides.
A program may use at most 64 MiB of HBM per device.

v0:
```python
import math
import jax
import jax.numpy as jnp
from jax import lax
from jax.sharding import PartitionSpec as P

L = 64
LZ = 64
HIGHEST = lax.Precision.HIGHEST


def gamma_matrices(gamma_table):
    inserts = gamma_table.shape[0]
    columns = gamma_table[:, :, 0]
    powers = gamma_table[:, :, 1]
    spin_ids = jnp.arange(4, dtype=jnp.int32)
    matches = (columns[:, :, None] == spin_ids[None, None, :]).astype(jnp.float32)
    unit_re = (powers == 0).astype(jnp.float32) - (powers == 2).astype(jnp.float32)
    unit_im = (powers == 1).astype(jnp.float32) - (powers == 3).astype(jnp.float32)
    return (
        (matches * unit_re[:, :, None]).reshape(inserts, 16),
        (matches * unit_im[:, :, None]).reshape(inserts, 16),
    )


def dft_table(length, anchor):
    wavenum = jnp.arange(length, dtype=jnp.int32)
    offsets = jnp.mod(wavenum - anchor, length)
    phase_index = jnp.mod(offsets[:, None] * wavenum[None, :], length)
    angles = 2.0 * math.pi / length * phase_index.astype(jnp.float32)
    return (jnp.cos(angles), -jnp.sin(angles))


def complex_step(real_part, imag_part, table_re, table_im, pattern):
    out_re = jnp.einsum(pattern, real_part, table_re, precision=HIGHEST) - jnp.einsum(
        pattern, imag_part, table_im, precision=HIGHEST
    )
    out_im = jnp.einsum(pattern, real_part, table_im, precision=HIGHEST) + jnp.einsum(
        pattern, imag_part, table_re, precision=HIGHEST
    )
    return (out_re, out_im)


def transform(fields, source_site):
    table_re, table_im = dft_table(fields.shape[4], source_site[2])
    along_z = jnp.stack(
        complex_step(fields[:, 0], fields[:, 1], table_re, table_im, "nabz,zk->nabk"), 1
    )
    depth_share = along_z.shape[4] // lax.axis_size("sy")
    first_depth = lax.axis_index("sy") * depth_share
    length_y = along_z.shape[3] * lax.axis_size("sy")
    full_re, full_im = dft_table(length_y, source_site[1])
    part = lax.dynamic_slice_in_dim(
        lax.all_gather(along_z, "sy", axis=3, tiled=True), first_depth, depth_share, 4
    )
    step_re, step_im = complex_step(part[:, 0], part[:, 1], full_re, full_im, "nayc,yk->nakc")
    along_y = jnp.stack([step_re, step_im], 1)
    arrived = lax.all_to_all(along_y, "sx", split_axis=3, concat_axis=2, tiled=True)
    table_re, table_im = dft_table(arrived.shape[2], source_site[0])
    along_x = complex_step(arrived[:, 0], arrived[:, 1], table_re, table_im, "nxbc,xk->nbck")
    return jnp.stack(along_x, 1)


def apply_gammas(mat_re, mat_im, real_part, imag_part):
    extent = real_part.shape
    flat_re = real_part.reshape(extent[0], -1)
    flat_im = imag_part.reshape(extent[0], -1)
    out_re = jnp.dot(mat_re, flat_re, precision=HIGHEST) - jnp.dot(
        mat_im, flat_im, precision=HIGHEST
    )
    out_im = jnp.dot(mat_re, flat_im, precision=HIGHEST) + jnp.dot(
        mat_im, flat_re, precision=HIGHEST
    )
    return (out_re.reshape(extent), out_im.reshape(extent))


def project_sites(fields, source_site, momenta, rows_x, rows_y, length, depth):
    coord_x = lax.axis_index("sx") * rows_x + jnp.arange(rows_x, dtype=jnp.int32) - source_site[0]
    coord_y = lax.axis_index("sy") * rows_y + jnp.arange(rows_y, dtype=jnp.int32) - source_site[1]
    coord_z = jnp.arange(depth, dtype=jnp.int32) - source_site[2]
    part_x = jnp.mod(momenta[:, 0:1] * coord_x[None, :], length)
    part_y = jnp.mod(momenta[:, 1:2] * coord_y[None, :], length)
    part_z = jnp.mod(momenta[:, 2:3] * coord_z[None, :], depth)
    plane = jnp.mod(part_x[:, :, None] + part_y[:, None, :], length).astype(jnp.float32)
    angles = (
        2.0 * math.pi / length * plane[:, :, :, None]
        + 2.0 * math.pi / depth * part_z.astype(jnp.float32)[:, None, None, :]
    )
    angles = angles.reshape(momenta.shape[0], -1)
    cosine = jnp.cos(angles)
    sine = jnp.sin(angles)
    field_re = fields[:, 0].reshape(fields.shape[0], -1)
    field_im = fields[:, 1].reshape(fields.shape[0], -1)
    local_re = jnp.dot(field_re, cosine.T, precision=HIGHEST) + jnp.dot(
        field_im, sine.T, precision=HIGHEST
    )
    local_im = jnp.dot(field_im, cosine.T, precision=HIGHEST) - jnp.dot(
        field_re, sine.T, precision=HIGHEST
    )
    return (local_re, local_im)


def body(forward_prop, backward_prop, gamma_table, source_site, momenta):
    slices = forward_prop.shape[0]
    rows_x = forward_prop.shape[4]
    rows_y = backward_prop.shape[5] // LZ
    inserts = gamma_table.shape[0]
    forward = forward_prop.reshape(slices, 2, 4, 3, 12, -1)
    backward = backward_prop.reshape(slices, 2, 4, 3, 12, -1)
    pattern = "tscjn,tucjn->sutn"
    pair_re = jnp.einsum(
        pattern, backward[:, 0], forward[:, 0], preferred_element_type=jnp.float32
    ) + jnp.einsum(pattern, backward[:, 1], forward[:, 1], preferred_element_type=jnp.float32)
    pair_im = jnp.einsum(
        pattern, backward[:, 0], forward[:, 1], preferred_element_type=jnp.float32
    ) - jnp.einsum(pattern, backward[:, 1], forward[:, 0], preferred_element_type=jnp.float32)
    pair_re = pair_re.reshape(16, slices, -1)
    pair_im = pair_im.reshape(16, slices, -1)
    mat_re, mat_im = gamma_matrices(gamma_table)
    field_re, field_im = apply_gammas(mat_re, mat_im, pair_re, pair_im)
    fields = jnp.stack([field_re, field_im], 2).reshape(inserts * slices, 2, rows_x, rows_y, LZ)
    spectrum = transform(fields, source_site)
    local_re, local_im = project_sites(fields, source_site, momenta, rows_x, rows_y, L, LZ)
    listed_re, listed_im = lax.psum((local_re, local_im), ("sx", "sy"))
    listed_re = listed_re.reshape(inserts, slices, -1)
    listed_im = listed_im.reshape(inserts, slices, -1)
    corr_re = spectrum[:, 0].reshape(inserts, slices, spectrum.shape[2], -1)
    corr_im = spectrum[:, 1].reshape(inserts, slices, spectrum.shape[2], -1)
    return (jnp.stack([corr_re, corr_im], 2), jnp.stack([listed_re, listed_im], 0))


def solution(mesh):
    placed = (
        P(None, None, None, None, "sx", "sy"),
        P(None, None, None, None, "sx", "sy"),
        P(),
        P(),
        P(),
    )
    return jax.shard_map(
        body,
        mesh=mesh,
        in_specs=placed,
        out_specs=(P(None, None, None, "sx", "sy"), P()),
        check_vma=False,
    )
```

profile of v0, /device:TPU:1, one launch (start us, length us, event | category | flops | bytes accessed | tf_op | source)
XLA Modules:
  0.0 323.4 jit_solution(12954592644119887692)
XLA Ops:
  7.2 0.7 fusion.92
  7.9 2.1 reshape.371
  10.0 0.8 fusion.144
  10.9 4.5 %copy.82 = bf16[2,1,4,3,12,512]{4,2,3,5,0,1:T(4,128)(2,1)S(1)} copy(bf16[2,1,4,3,12,512]{5,4,3,2,1,0:T(8,128)(2,1)} %get-tuple-element.11) | data formatting | bytes 589824
  15.3 2.8 reshape.372
  18.1 2.1 fusion.145
  20.2 5.3 %copy.83 = bf16[2,1,4,3,12,512]{4,2,3,5,0,1:T(4,128)(2,1)} copy(bf16[2,1,4,3,12,512]{5,4,3,2,1,0:T(8,128)(2,1)} %get-tuple-element.13) | data formatting | bytes 589824
  25.4 3.8 %copy.80 = bf16[2,1,4,3,12,512]{4,2,3,5,0,1:T(4,128)(2,1)} copy(bf16[2,1,4,3,12,512]{5,4,3,2,1,0:T(8,128)(2,1)S(1)} %get-tuple-element.10) | data formatting | bytes 589824
  29.2 5.3 %copy.81 = bf16[2,1,4,3,12,512]{4,2,3,5,0,1:T(4,128)(2,1)} copy(bf16[2,1,4,3,12,512]{5,4,3,2,1,0:T(8,128)(2,1)} %get-tuple-element.12) | data formatting | bytes 589824
  34.5 5.6 %fusion.2 = f32[2,512,4,4,1]{3,2,4,1,0:T(4,128)S(1)} fusion(bf16[2,1,4,3,12,512]{4,2,3,5,0,1:T(4,128)(2,1)} %copy.83, bf16[2,1,4,3,12,512]{4,2,3,5,0,1:T(4,128)(2,1)S(1)} %copy.82), kind=kOutput, calls=%fused_computation.2 | convolution fusion | flops 1179648 | bytes 655360 | tf_op jit(solution)/shard_map/tscjn,tucjn->sutn/dot_general | solution.py:113
  40.2 5.0 %fusion = f32[2,512,4,4,1]{3,2,4,1,0:T(4,128)} fusion(bf16[2,1,4,3,12,512]{4,2,3,5,0,1:T(4,128)(2,1)S(1)} %copy-done.1, bf16[2,1,4,3,12,512]{4,2,3,5,0,1:T(4,128)(2,1)S(1)} %copy-done.2), kind=kOutput, calls=%fused_computation | convolution fusion | flops 1179648 | bytes 655360 | tf_op jit(solution)/shard_map/tscjn,tucjn->sutn/dot_general | solution.py:116
  45.2 3.7 %fusion.13 = f32[4,4,2,512]{0,1,3,2:T(4,128)} fusion(f32[2,512,4,4,1]{3,2,4,1,0:T(4,128)S(1)} %fusion.2, bf16[2,1,4,3,12,512]{4,2,3,5,0,1:T(4,128)(2,1)S(1)} %copy-done, bf16[2,1,4,3,12,512]{4,2,3,5,0,1:T(4,128)(2,1)S(1)} %copy-done.2), kind=kOutput, calls=%fused_computation.17 | convolution fusion | flops 1196032 | bytes 720896 | tf_op jit(solution)/shard_map/tscjn,tucjn->sutn/dot_general | solution.py:111
  48.8 2.1 copy.48
  51.0 7.5 %fusion.12 = f32[4,4,2,512]{0,1,3,2:T(4,128)} fusion(f32[2,512,4,4,1]{3,2,4,1,0:T(4,128)} %fusion, bf16[2,1,4,3,12,512]{4,2,3,5,0,1:T(4,128)(2,1)} %copy.81, bf16[2,1,4,3,12,512]{4,2,3,5,0,1:T(4,128)(2,1)S(1)} %copy.82), kind=kOutput, calls=%fused_computation.15 | convolution fusion | flops 1196032 | bytes 720896 | tf_op jit(solution)/shard_map/tscjn,tucjn->sutn/dot_general | solution.py:114
  58.5 1.9 copy.49
  60.5 0.7 fusion.146
  62.0 1.3 and_select_fusion.1
  63.3 0.5 fusion.32
  63.8 0.5 fusion.30
  64.6 0.5 fusion.25
  65.1 0.5 fusion.24
  65.5 0.7 pad_maximum_fusion
  66.3 0.6 iota_subtract_fusion
  67.0 0.7 add_subtract_fusion.1
  67.6 0.7 add_subtract_fusion
  68.7 1.1 add_sine_fusion
  70.0 0.7 and_select_fusion.3
  71.1 107.5 %all-gather.2.cloned.1.call-done = f32[32,2,2,64,64]{4,0,3,2,1:T(8,128)} async-done(((f32[32,2,2,4,64]{4,0,3,2,1:T(8,128)}), f32[32,2,2,64,64]{4,0,3,2,1:T(8,128)}) %all-gather.2.cloned.1.call-update) | async-done | bytes 2097168 | tf_op jit(solution)/shard_map/all_gather | solution.py:54
  178.6 4.7 %dynamic-slice_bitcast_fusion = (f32[32,2,64,4]{3,0,2,1:T(8,128)S(1)}, f32[32,2,64,4]{3,0,2,1:T(8,128)}) fusion(f32[32,2,2,64,64]{4,0,3,2,1:T(8,128)} %all-gather.2.cloned.1.call-done, s32[]{:T(128)S(6)} %add.213, s32[]{:T(128)S(6)} %select_n.88), kind=kLoop, calls=%fused_computation.12 | loop fusion | bytes 262152 | tf_op jit(solution)/shard_map/squeeze | solution.py:56
  183.3 2.6 copy.54
  186.0 0.5 fusion.51
  186.4 0.5 fusion.53
  186.9 1.2 copy.55
  188.1 0.5 fusion.23
  188.5 0.5 fusion.22
  189.0 0.3 copy.58
  189.4 1.0 reshape.373
  190.4 13.0 %all-to-all-start = ((f32[32,1,1024]{2,1,0:T(1,128)}), f32[32,1,1024]{2,1,0:T(1,128)S(1)}, u32[]{:S(2)}, u32[]{:S(2)}) async-start(f32[32,1,1024]{2,1,0:T(1,128)} %reshape.373), calls=%async_computation | async-start | bytes 262144 | tf_op jit(solution)/shard_map/all_to_all | solution.py:58
  203.8 106.2 %all-reduce = (f32[1,16,2,32]{3,2,1,0:T(2,128)S(1)}, f32[1,16,2,32]{3,2,1,0:T(2,128)S(1)}) all-reduce(f32[1,16,2,32]{3,2,1,0:T(2,128)S(1)} %bitcast.184, f32[1,16,2,32]{3,2,1,0:T(2,128)S(1)} %bitcast.183), channel_id=1, replica_groups=mesh['sx'=32,'sy'=16] {'sx','sy'}, use_global_device_ids=true, to_apply=%region_1.2 | all-reduce | flops 2048 | bytes 16384 | tf_op jit(solution)/shard_map/psum | solution.py:124
  309.9 0.6 pad_maximum_fusion.3
  310.6 0.5 broadcast.522
  311.1 0.9 reduce
  312.5 0.4 copy.60
  312.9 0.6 fusion.27
  313.5 0.6 fusion.26
  314.1 0.6 convolution_subtract_fusion.2
  315.0 0.6 convolution_add_fusion.2
  315.9 0.7 copy.65
  (45 shorter events, 3.7 us)
Async XLA Ops:
  7.2 171.4 %all-gather.2.cloned.1.call-start = ((), (), s32[]{:S(2)}) async-start(), calls=%async_computation.1 | async-start | bytes 4456448 | tf_op jit(solution)/shard_map/all_gather | solution.py:54
  34.5 5.6 %copy-start.1 = (bf16[2,1,4,3,12,512]{4,2,3,5,0,1:T(4,128)(2,1)S(1)}, bf16[2,1,4,3,12,512]{4,2,3,5,0,1:T(4,128)(2,1)}, u32[]{:S(2)}) copy-start(bf16[2,1,4,3,12,512]{4,2,3,5,0,1:T(4,128)(2,1)} %copy.83) | copy-start | bytes 884740
  34.5 5.6 %copy-start.2 = (bf16[2,1,4,3,12,512]{4,2,3,5,0,1:T(4,128)(2,1)S(1)}, bf16[2,1,4,3,12,512]{4,2,3,5,0,1:T(4,128)(2,1)}, u32[]{:S(2)}) copy-start(bf16[2,1,4,3,12,512]{4,2,3,5,0,1:T(4,128)(2,1)} %copy.80) | copy-start | bytes 884740
  40.2 5.0 %copy-start = (bf16[2,1,4,3,12,512]{4,2,3,5,0,1:T(4,128)(2,1)S(1)}, bf16[2,1,4,3,12,512]{4,2,3,5,0,1:T(4,128)(2,1)}, u32[]{:S(2)}) copy-start(bf16[2,1,4,3,12,512]{4,2,3,5,0,1:T(4,128)(2,1)} %copy.81) | copy-start | bytes 884740
  50.9 9.5 %copy-start.3 = (s32[3]{0:T(128)S(1)}, s32[3]{0:T(128)}, u32[]{:S(2)}) copy-start(s32[3]{0:T(128)} %param.8) | copy-start | bytes 40
  50.9 10.2 %slice-start = ((s32[16,4,2]{0,2,1:T(2,128)}), s32[16,4,1]{0,2,1:T(1,128)S(1)}, s32[]{:S(2)}) async-start(s32[16,4,2]{0,2,1:T(2,128)} %param.7), calls=%async_computation.2 | async-start | bytes 4096 | tf_op jit(solution)/shard_map/slice | solution.py:14
  58.5 9.8 %copy-start.4 = (s32[32,3]{0,1:T(4,128)S(1)}, s32[32,3]{0,1:T(4,128)}, u32[]{:S(2)}) copy-start(s32[32,3]{0,1:T(4,128)} %param.9) | copy-start | bytes 1156
  190.4 120.2 %all-to-all-start = ((f32[32,1,1024]{2,1,0:T(1,128)}), f32[32,1,1024]{2,1,0:T(1,128)S(1)}, u32[]{:S(2)}, u32[]{:S(2)}) async-start(f32[32,1,1024]{2,1,0:T(1,128)} %reshape.373), calls=%async_computation | async-start | bytes 262144 | tf_op jit(solution)/shard_map/all_to_all | solution.py:58
Sparse Core Ops, SparseCore 0:
  66.4 112.1 all-gather.1
where the time goes:
time: 325 us; the launch traced here: 323 us
  waiting for transfers between devices  108 us (33%)
  blocking collectives  106 us (33%)
  local copies, waits for them, and re-layouts  44.1 us (14%)
  matrix products  29.7 us (9%)
  between operations  14.4 us (4%)
  starting transfers between devices  13 us (4%)
  other arithmetic  8.45 us (3%)
    all_gather x1, waiting for transfers between devices, transform(): lax.all_gather(along_z, 'sy', axis=3, tiled=True)  107 us
    psum x1, blocking collectives, body(): listed_re, listed_im = lax.psum((local_re, local_im), ('sx', 'sy'))  106 us
    unnamed x19, local copies, waits for them, and re-layouts  20.8 us
    all_to_all x1, starting transfers between devices, transform(): lax.all_to_all(along_y, 'sx', split_axis=3, concat_axis=2, tiled=True)  13 us
    dot_general x1, matrix products, body(): jnp.einsum(pattern, backward[:, 0], forward[:, 1], preferred_element_type...  7.53 us
  transfers between devices with their start and end apart: 2, of which 1 were waited for; matrix products, arithmetic and copies ran while one was open for 2% of the time, Pallas kernels for 0%

commit v1 on v0

--- a/solution.py
+++ b/solution.py
@@ -7,6 +7,11 @@
 L = 64
 LZ = 64
 HIGHEST = lax.Precision.HIGHEST
+
+
+def _detail_zone(matrix):
+    arr_out = jax.lax.psum(matrix, axis_name="sy")
+    return jax.lax.psum(arr_out, axis_name="sx")
 
 
 def gamma_matrices(gamma_table):
@@ -121,7 +126,7 @@
     fields = jnp.stack([field_re, field_im], 2).reshape(inserts * slices, 2, rows_x, rows_y, LZ)
     spectrum = transform(fields, source_site)
     local_re, local_im = project_sites(fields, source_site, momenta, rows_x, rows_y, L, LZ)
-    listed_re, listed_im = lax.psum((local_re, local_im), ("sx", "sy"))
+    listed_re, listed_im = _detail_zone((local_re, local_im))
     listed_re = listed_re.reshape(inserts, slices, -1)
     listed_im = listed_im.reshape(inserts, slices, -1)
     corr_re = spectrum[:, 0].reshape(inserts, slices, spectrum.shape[2], -1)

time: 325 us -> 461 us (1.42); the launches traced: 323 us -> 454 us
  blocking collectives: 106 us -> 237 us
    psum x1 -> x2, blocking collectives: 106 us -> 237 us  [the longest x1 172 us: _detail_zone(): return jax.lax.psum(arr_out, axis_name='sx')]
  transfers between devices with their start and end apart: 2 -> 2, of which waited for: 1 -> 1; matrix products, arithmetic and copies ran while one was open for 2% -> 1% of each run, Pallas kernels for 0% -> 0%
where the time goes in v1:
time: 461 us; the launch traced here: 454 us
  blocking collectives  237 us (51%)
  waiting for transfers between devices  108 us (23%)
  local copies, waits for them, and re-layouts  44.1 us (10%)
  matrix products  29.8 us (6%)
  between operations  14.4 us (3%)
  starting transfers between devices  13 us (3%)
  other arithmetic  8.31 us (2%)
    psum x1, blocking collectives, _detail_zone(): return jax.lax.psum(arr_out, axis_name='sx')  172 us
    all_gather x1, waiting for transfers between devices, transform(): lax.all_gather(along_z, 'sy', axis=3, tiled=True)  108 us
    psum x1, blocking collectives, _detail_zone(): arr_out = jax.lax.psum(matrix, axis_name='sy')  64.9 us
    unnamed x19, local copies, waits for them, and re-layouts  20.8 us
    all_to_all x1, starting transfers between devices, transform(): lax.all_to_all(along_y, 'sx', split_axis=3, concat_axis=2, tiled=True)  13 us
  transfers between devices with their start and end apart: 2, of which 1 were waited for; matrix products, arithmetic and copies ran while one was open for 1% of the time, Pallas kernels for 0%

profile of v1, /device:TPU:1, one launch (start us, length us, event | category | flops | bytes accessed | tf_op | source)
XLA Modules:
  0.0 454.5 jit_solution(13888553859849619301)
XLA Ops:
  7.2 0.7 fusion.92
  7.9 2.1 reshape.371
  10.0 0.8 fusion.144
  10.8 4.5 copy.82
  15.3 2.8 reshape.372
  18.1 2.1 fusion.145
  20.2 5.3 %copy.83 = bf16[2,1,4,3,12,512]{4,2,3,5,0,1:T(4,128)(2,1)} copy(bf16[2,1,4,3,12,512]{5,4,3,2,1,0:T(8,128)(2,1)} %get-tuple-element.15) | data formatting | bytes 589824
  25.5 3.8 copy.80
  29.3 5.3 %copy.81 = bf16[2,1,4,3,12,512]{4,2,3,5,0,1:T(4,128)(2,1)} copy(bf16[2,1,4,3,12,512]{5,4,3,2,1,0:T(8,128)(2,1)} %get-tuple-element.14) | data formatting | bytes 589824
  34.6 5.6 %fusion.2 = f32[2,512,4,4,1]{3,2,4,1,0:T(4,128)S(1)} fusion(bf16[2,1,4,3,12,512]{4,2,3,5,0,1:T(4,128)(2,1)} %copy.83, bf16[2,1,4,3,12,512]{4,2,3,5,0,1:T(4,128)(2,1)S(1)} %copy.82), kind=kOutput, calls=%fused_computation.2 | convolution fusion | flops 1179648 | bytes 655360 | tf_op jit(solution)/shard_map/tscjn,tucjn->sutn/dot_general | solution.py:118
  40.2 5.0 %fusion = f32[2,512,4,4,1]{3,2,4,1,0:T(4,128)} fusion(bf16[2,1,4,3,12,512]{4,2,3,5,0,1:T(4,128)(2,1)S(1)} %copy-done.1, bf16[2,1,4,3,12,512]{4,2,3,5,0,1:T(4,128)(2,1)S(1)} %copy-done.2), kind=kOutput, calls=%fused_computation | convolution fusion | flops 1179648 | bytes 655360 | tf_op jit(solution)/shard_map/tscjn,tucjn->sutn/dot_general | solution.py:121
  45.2 3.7 fusion.13
  48.9 2.1 copy.48
  51.0 7.5 %fusion.12 = f32[4,4,2,512]{0,1,3,2:T(4,128)} fusion(f32[2,512,4,4,1]{3,2,4,1,0:T(4,128)} %fusion, bf16[2,1,4,3,12,512]{4,2,3,5,0,1:T(4,128)(2,1)} %copy.81, bf16[2,1,4,3,12,512]{4,2,3,5,0,1:T(4,128)(2,1)S(1)} %copy.82), kind=kOutput, calls=%fused_computation.15 | convolution fusion | flops 1196032 | bytes 720896 | tf_op jit(solution)/shard_map/tscjn,tucjn->sutn/dot_general | solution.py:119
  58.6 1.9 copy.49
  60.5 0.6 fusion.146
  62.0 1.2 and_select_fusion.1
  63.2 0.5 fusion.32
  63.7 0.5 fusion.30
  64.5 0.5 fusion.25
  65.0 0.5 fusion.24
  65.5 0.7 pad_maximum_fusion
  66.3 0.6 iota_subtract_fusion
  66.8 0.7 add_subtract_fusion.1
  67.5 0.7 add_subtract_fusion
  68.6 1.1 add_sine_fusion
  69.9 0.7 and_select_fusion.3
  71.0 107.6 %all-gather.2.cloned.1.call-done = f32[32,2,2,64,64]{4,0,3,2,1:T(8,128)} async-done(((f32[32,2,2,4,64]{4,0,3,2,1:T(8,128)}), f32[32,2,2,64,64]{4,0,3,2,1:T(8,128)}) %all-gather.2.cloned.1.call-update) | async-done | bytes 2097168 | tf_op jit(solution)/shard_map/all_gather | solution.py:59
  178.6 4.7 %dynamic-slice_bitcast_fusion = (f32[32,2,64,4]{3,0,2,1:T(8,128)S(1)}, f32[32,2,64,4]{3,0,2,1:T(8,128)}) fusion(f32[32,2,2,64,64]{4,0,3,2,1:T(8,128)} %all-gather.2.cloned.1.call-done, s32[]{:T(128)S(6)} %add.217, s32[]{:T(128)S(6)} %select_n.88), kind=kLoop, calls=%fused_computation.12 | loop fusion | bytes 262152 | tf_op jit(solution)/shard_map/squeeze | solution.py:61
  183.2 2.6 copy.54
  185.9 0.5 fusion.51
  186.3 0.5 fusion.53
  186.8 1.2 copy.55
  188.0 0.5 fusion.23
  188.5 0.5 fusion.22
  189.3 1.0 reshape.373
  190.3 13.0 %all-to-all-start = ((f32[32,1,1024]{2,1,0:T(1,128)}), f32[32,1,1024]{2,1,0:T(1,128)S(1)}, u32[]{:S(2)}, u32[]{:S(2)}) async-start(f32[32,1,1024]{2,1,0:T(1,128)} %reshape.373), calls=%async_computation | async-start | bytes 262144 | tf_op jit(solution)/shard_map/all_to_all | solution.py:63
  203.7 64.9 %all-reduce.1 = (f32[32,32]{1,0:T(8,128)S(1)}, f32[32,32]{1,0:T(8,128)S(1)}) all-reduce(f32[32,32]{1,0:T(8,128)S(1)} %convolution_subtract_fusion.4, f32[32,32]{1,0:T(8,128)S(1)} %convolution_add_fusion.4), channel_id=1, replica_groups=mesh['sx'=32,'sy'=16] {'sy'}, use_global_device_ids=true, to_apply=%region_2.3 | all-reduce | flops 2048 | bytes 16384 | tf_op jit(solution)/shard_map/psum | solution.py:13
  268.6 172.4 %all-reduce = (f32[1,16,2,32]{3,2,1,0:T(2,128)S(1)}, f32[1,16,2,32]{3,2,1,0:T(2,128)S(1)}) all-reduce(f32[1,16,2,32]{3,2,1,0:T(2,128)S(1)} %bitcast.183, f32[1,16,2,32]{3,2,1,0:T(2,128)S(1)} %bitcast.184), channel_id=1, replica_groups=mesh['sx'=32,'sy'=16] {'sx'}, use_global_device_ids=true, to_apply=%region_3.4 | all-reduce | flops 2048 | bytes 16384 | tf_op jit(solution)/shard_map/psum | solution.py:14
  440.9 0.6 pad_maximum_fusion.3
  441.6 0.5 broadcast.522
  442.1 0.9 reduce
  443.5 0.4 copy.60
  443.9 0.6 fusion.27
  444.5 0.6 fusion.26
  445.2 0.6 convolution_subtract_fusion.2
  446.0 0.6 convolution_add_fusion.2
  446.9 0.7 copy.65
  (46 shorter events, 4.1 us)
Async XLA Ops:
  7.2 171.4 %all-gather.2.cloned.1.call-start = ((), (), s32[]{:S(2)}) async-start(), calls=%async_computation.1 | async-start | bytes 4456448 | tf_op jit(solution)/shard_map/all_gather | solution.py:59
  34.5 5.6 %copy-start.1 = (bf16[2,1,4,3,12,512]{4,2,3,5,0,1:T(4,128)(2,1)S(1)}, bf16[2,1,4,3,12,512]{4,2,3,5,0,1:T(4,128)(2,1)}, u32[]{:S(2)}) copy-start(bf16[2,1,4,3,12,512]{4,2,3,5,0,1:T(4,128)(2,1)} %copy.83) | copy-start | bytes 884740
  34.6 5.6 %copy-start.2 = (bf16[2,1,4,3,12,512]{4,2,3,5,0,1:T(4,128)(2,1)S(1)}, bf16[2,1,4,3,12,512]{4,2,3,5,0,1:T(4,128)(2,1)}, u32[]{:S(2)}) copy-start(bf16[2,1,4,3,12,512]{4,2,3,5,0,1:T(4,128)(2,1)} %copy.80) | copy-start | bytes 884740
  40.2 5.0 %copy-start = (bf16[2,1,4,3,12,512]{4,2,3,5,0,1:T(4,128)(2,1)S(1)}, bf16[2,1,4,3,12,512]{4,2,3,5,0,1:T(4,128)(2,1)}, u32[]{:S(2)}) copy-start(bf16[2,1,4,3,12,512]{4,2,3,5,0,1:T(4,128)(2,1)} %copy.81) | copy-start | bytes 884740
  51.0 9.5 %copy-start.3 = (s32[3]{0:T(128)S(1)}, s32[3]{0:T(128)}, u32[]{:S(2)}) copy-start(s32[3]{0:T(128)} %param.8) | copy-start | bytes 40
  51.0 10.1 %slice-start = ((s32[16,4,2]{0,2,1:T(2,128)}), s32[16,4,1]{0,2,1:T(1,128)S(1)}, s32[]{:S(2)}) async-start(s32[16,4,2]{0,2,1:T(2,128)} %param.7), calls=%async_computation.2 | async-start | bytes 4096 | tf_op jit(solution)/shard_map/slice | solution.py:19
  58.6 9.6 %copy-start.4 = (s32[32,3]{0,1:T(4,128)S(1)}, s32[32,3]{0,1:T(4,128)}, u32[]{:S(2)}) copy-start(s32[32,3]{0,1:T(4,128)} %param.9) | copy-start | bytes 1156
  190.3 251.3 %all-to-all-start = ((f32[32,1,1024]{2,1,0:T(1,128)}), f32[32,1,1024]{2,1,0:T(1,128)S(1)}, u32[]{:S(2)}, u32[]{:S(2)}) async-start(f32[32,1,1024]{2,1,0:T(1,128)} %reshape.373), calls=%async_computation | async-start | bytes 262144 | tf_op jit(solution)/shard_map/all_to_all | solution.py:63
Sparse Core Ops, SparseCore 0:
  66.3 112.1 all-gather.1
